TPU v7x, 128 devices: a whole 4x4x4 slice. The times are simulated.
128 devices in a mesh: fsdp: 32 (over z, y, core), slide: 4 (over x).
Axes of the slice: x: 4, y: 4, z: 4, core: 2. Of those that a mesh axis runs over, the one named last changes fastest.
Arguments:
- tiles: bfloat16 [65536, 1536], P(('slide', 'fsdp')), parts along dimension 0, may hold values from -6 to 6
- tile_cell: int32 [65536], P('slide'), parts along dimension 0, may hold values from 0 to 16383, as said below
- tissue: int32 [256, 256], P('slide'), parts along dimension 0, may hold values 0 or 1
- norm_gain: float32 [2, 1536], replicated, may hold values from 0.5 to 1.5
- qk_gain: float32 [2, 2, 64], replicated, may hold values from 0.5 to 4
- row_qkv: bfloat16 [1536, 4608], P(None, 'fsdp'), may hold values from -0.15625 to 0.15625
- row_out: bfloat16 [1536, 1536], P(None, 'fsdp'), may hold values from -0.15625 to 0.15625
- col_qkv: bfloat16 [1536, 4608], P(None, 'fsdp'), may hold values from -0.15625 to 0.15625
- col_out: bfloat16 [1536, 1536], P(None, 'fsdp'), may hold values from -0.15625 to 0.15625
Outputs:
- encoded: bfloat16 [256, 256, 1536], P('slide', 'fsdp'), parts along dimension 0
There are 4 independent parts, one for each index of `slide`. A program takes and returns all parts, laid end to end along the dimension named above; an argument that names none is the same for every part. Nothing has to cross between parts.
Inputs may be any that keep to these rules, and one draw needn't show every extreme that they name: Slots d * 512 + b * 16 up to d * 512 + (b + 1) * 16 - 1 hold tiles of grid rows b * 2 to (b + 1) * 2 - 1; tile_cell names every grid cell exactly once.
All inputs are finite; a program needn't handle non-finite values.
Results may differ from a plain program's by a relative error of at most 0.02.
The roundings to bfloat16 on the way count: a program that leaves them out, or rounds other values in their place, can miss the bound.
Values may be sent and summed in bfloat16 or wider, within the bound.
No kernel may reach another device: no remote copies, remote signals or barrier semaphores. Data moves between devices by JAX's collectives and lax.ppermute only.
A program may use at most 256 MiB of HBM per device.

v0:
```python
import jax
import jax.numpy as jnp
from jax import lax
from jax.sharding import PartitionSpec as P

HEADS = 24
EPS = 1e-06


def rms_norm(grid, gain):
    values = grid.astype(jnp.float32)
    scale = lax.rsqrt(jnp.mean(values * values, axis=-1, keepdims=True) + EPS)
    return (values * scale * gain).astype(jnp.bfloat16)


def head_norm(values, gain):
    scale = lax.rsqrt(jnp.mean(values * values, axis=-1, keepdims=True) + EPS)
    return values * scale * gain


def rotate(values, rows_pos, cols_pos):
    quarter = values.shape[-1] // 4
    freq = 10000.0 ** (-jnp.arange(quarter).astype(jnp.float32) / quarter)

    def turn(part, position):
        angle = position.astype(jnp.float32)[..., None, None] * freq
        cosine = jnp.cos(angle)
        sine = jnp.sin(angle)
        first = part[..., :quarter]
        second = part[..., quarter:]
        return jnp.concatenate(
            [first * cosine - second * sine, first * sine + second * cosine], axis=-1
        )

    half = 2 * quarter
    return jnp.concatenate(
        [turn(values[..., :half], rows_pos), turn(values[..., half:], cols_pos)], axis=-1
    )


def attend(qkv, gains, rows_pos, cols_pos, keys_live, column, heads):
    width = qkv.shape[-1] // 3
    size = width // heads
    shape = qkv.shape[:-1] + (heads, size)
    query = qkv[..., :width].reshape(shape).astype(jnp.float32)
    key = qkv[..., width : 2 * width].reshape(shape).astype(jnp.float32)
    value = qkv[..., 2 * width :].reshape(shape)
    query = rotate(head_norm(query, gains[0]), rows_pos, cols_pos).astype(jnp.bfloat16)
    key = rotate(head_norm(key, gains[1]), rows_pos, cols_pos).astype(jnp.bfloat16)
    if column:
        score_form = "lbhd,mbhd->bhlm"
        mix_form = "bhlm,mbhd->lbhd"
        live = keys_live.T
    else:
        score_form = "blhd,bmhd->bhlm"
        mix_form = "bhlm,bmhd->blhd"
        live = keys_live
    scores = jnp.einsum(score_form, query, key, preferred_element_type=jnp.float32) * size ** (-0.5)
    length = scores.shape[-1]
    diagonal = jnp.arange(length)[:, None] == jnp.arange(length)[None, :]
    allow = (live[:, None, None, :] > 0) | diagonal[None, None]
    scores = jnp.where(allow, scores, -1e30)
    top = jnp.max(scores, axis=-1, keepdims=True)
    weights = jnp.exp(scores - top)
    total = jnp.sum(weights, axis=-1)
    mixed = jnp.einsum(
        mix_form, weights.astype(jnp.bfloat16), value, preferred_element_type=jnp.float32
    )
    if column:
        total = total.transpose(2, 0, 1)
    else:
        total = total.transpose(0, 2, 1)
    return (mixed / total[..., None]).reshape(qkv.shape[:-1] + (width,)).astype(jnp.bfloat16)


def project_qkv(normed, weight):

    def multiply(piece, start):
        return jnp.dot(normed, piece, preferred_element_type=jnp.float32)

    return multiply(lax.all_gather(weight, "fsdp", axis=1, tiled=True), jnp.int32(0)).astype(
        jnp.bfloat16
    )


def project_out(mixed, weight):

    def multiply(piece, start):
        return jnp.dot(mixed, piece, preferred_element_type=jnp.float32)

    return multiply(lax.all_gather(weight, "fsdp", axis=1, tiled=True), jnp.int32(0))


def on_device(tiles, tile_cell, tissue, norm_gain, qk_gain, row_qkv, row_out, col_qkv, col_out):
    count = lax.axis_size("fsdp")
    index = lax.axis_index("fsdp")
    width = tiles.shape[1]
    tok_dev = tiles.shape[0]
    slots = tok_dev // count
    grid_rows = tissue.shape[0]
    columns = tissue.shape[1]
    rows_dev = grid_rows // count
    cols_dev = columns // count
    arrived = lax.all_to_all(
        tiles.reshape(count, slots, width), "fsdp", split_axis=0, concat_axis=0, tiled=True
    )
    table_cell = lax.dynamic_index_in_dim(
        tile_cell.reshape(count, count, slots), index, 1, keepdims=False
    )
    row_base = index * rows_dev
    local_cells = (table_cell - row_base * columns).reshape(-1)
    grid = (
        jnp.zeros((tok_dev, width), jnp.bfloat16)
        .at[local_cells]
        .set(arrived.reshape(tok_dev, width))
    )
    rows_pos = row_base + lax.broadcasted_iota(jnp.int32, (rows_dev, columns), 0)
    cols_pos = lax.broadcasted_iota(jnp.int32, (rows_dev, columns), 1)
    live_rows = lax.dynamic_slice_in_dim(tissue, row_base, rows_dev, 0)
    qkv = project_qkv(rms_norm(grid, norm_gain[0]), row_qkv).reshape(rows_dev, columns, 3 * width)
    mixed = attend(qkv, qk_gain[0], rows_pos, cols_pos, live_rows, False, HEADS)
    hidden = grid.astype(jnp.float32) + project_out(mixed.reshape(tok_dev, width), row_out)
    hidden = hidden.astype(jnp.bfloat16).reshape(rows_dev, columns, width)
    turned = lax.all_to_all(hidden, "fsdp", split_axis=1, concat_axis=0, tiled=True)
    col_base = index * cols_dev
    rows_pos_col = lax.broadcasted_iota(jnp.int32, (grid_rows, cols_dev), 0)
    cols_pos_col = col_base + lax.broadcasted_iota(jnp.int32, (grid_rows, cols_dev), 1)
    live_cols = lax.dynamic_slice_in_dim(tissue, col_base, cols_dev, 1)
    flat = turned.reshape(grid_rows * cols_dev, width)
    qkv_col = project_qkv(rms_norm(flat, norm_gain[1]), col_qkv).reshape(
        grid_rows, cols_dev, 3 * width
    )
    mixed_col = attend(qkv_col, qk_gain[1], rows_pos_col, cols_pos_col, live_cols, True, HEADS)
    result = flat.astype(jnp.float32) + project_out(
        mixed_col.reshape(grid_rows * cols_dev, width), col_out
    )
    return result.astype(jnp.bfloat16).reshape(grid_rows, cols_dev, width)


def solution(mesh):
    return jax.shard_map(
        on_device,
        mesh=mesh,
        in_specs=(
            P(("slide", "fsdp"), None),
            P("slide"),
            P("slide", None),
            P(),
            P(),
            P(None, "fsdp"),
            P(None, "fsdp"),
            P(None, "fsdp"),
            P(None, "fsdp"),
        ),
        out_specs=P("slide", "fsdp", None),
        check_vma=False,
    )
```

profile of v0, /device:TPU:1, one launch (start us, length us, event | category | flops | bytes accessed | tf_op | source)
XLA Modules:
  0.0 325.4 jit_solution(16817885451585981338)
XLA Ops:
  8.8 9.6 %all-to-all-start = ((bf16[32,16,1536]{2,1,0:T(8,128)(2,1)}), bf16[32,16,1536]{2,1,0:T(8,128)(2,1)S(1)}, u32[]{:S(2)}, u32[]{:S(2)}) async-start(bf16[32,16,1536]{2,1,0:T(8,128)(2,1)} %bitcast.73), calls=%async_computation | async-start | bytes 3145728 | tf_op jit(solution)/shard_map/all_to_all | solution.py:104
  19.3 27.7 %all-to-all-done = bf16[32,16,1536]{2,1,0:T(8,128)(2,1)S(1)} async-done(((bf16[32,16,1536]{2,1,0:T(8,128)(2,1)}), bf16[32,16,1536]{2,1,0:T(8,128)(2,1)S(1)}, u32[]{:S(2)}, u32[]{:S(2)}) %all-to-all-start) | async-done | bytes 1572896 | tf_op jit(solution)/shard_map/all_to_all | solution.py:104
  46.9 3.4 %scatter_custom_fusion = bf16[512,1536]{1,0:T(8,128)(2,1)S(1)} fusion(s32[512]{0:T(512)S(1)} %bitcast.80, bf16[512,1536]{1,0:T(8,128)(2,1)S(1)} %bitcast.74, bf16[]{:T(256)} %constant.19.clone.1), kind=kCustom, calls=%fused_computation.104 | custom fusion | bytes 1572866 | tf_op jit(solution)/shard_map/scatter | solution.py:115
  50.8 38.5 %all-gather.5.cloned.1.call-done = bf16[1536,4608]{0,1:T(8,128)(2,1)} async-done(((bf16[1536,144]{0,1:T(8,128)(2,1)}), bf16[1536,4608]{0,1:T(8,128)(2,1)}) %all-gather.5.cloned.1.call-update) | async-done | bytes 14155792 | tf_op jit(solution)/shard_map/all_gather | solution.py:81
  89.3 11.1 %convolution_convert_fusion.1 = bf16[512,4608]{1,0:T(8,128)(2,1)S(1)} fusion(bf16[1536,4608]{0,1:T(8,128)(2,1)} %all-gather.5.cloned.1.call-done, bf16[512,1536]{1,0:T(8,128)(2,1)S(1)} %scatter_custom_fusion, f32[1536]{0:T(1024)S(1)} %get-tuple-element.6, f32[512]{0:T(512)S(1)} %add_rsqrt_fusion.5), kind=kOutput, calls=%fused_computation.7 | convolution fusion | flops 7253262336 | bytes 20455424 | tf_op jit(solution)/shard_map/dot_general | solution.py:79
  100.4 3.2 slice_convert_fusion.2
  103.6 2.4 copy.65
  108.3 2.6 copy.64
  110.9 2.5 multiply_reduce_fusion.4
  118.5 3.1 fusion.1
  121.7 3.5 %fusion.38 = bf16[2,256,24,64]{1,3,2,0:T(8,128)(2,1)S(1)} fusion(bf16[2,256,24,64]{1,3,2,0:T(8,128)(2,1)S(1)} %bitcast.75, f32[2,24,256,256]{2,3,1,0:T(8,128)S(1)} %get-tuple-element.54, f32[2,24,256]{2,1,0:T(8,128)S(1)} %get-tuple-element.53, pred[2,256,256]{1,2,0:T(8,128)(4,1)S(1)} %broadcast_or_fusion, f32[2,256,24]{1,2,0:T(8,128)S(1)} %bitcast.79), kind=kOutput, calls=%fused_computation.62 | convolution fusion | flops 416808960 | bytes 15958016 | tf_op jit(solution)/shard_map/bhlm,bmhd->blhd/dot_general | solution.py:66
  127.1 10.6 %all-gather.7.cloned.1.call-done = bf16[1536,1536]{0,1:T(8,128)(2,1)} async-done(((bf16[1536,48]{0,1:T(8,128)(2,1)}), bf16[1536,1536]{0,1:T(8,128)(2,1)}) %all-gather.7.cloned.1.call-update) | async-done | bytes 4718608 | tf_op jit(solution)/shard_map/all_gather | solution.py:91
  137.8 5.0 %fusion.44 = bf16[512,1536]{1,0:T(8,128)(2,1)S(1)} fusion(bf16[512,1536]{0,1:T(8,128)(2,1)S(1)} %bitcast.76, bf16[1536,1536]{0,1:T(8,128)(2,1)} %all-gather.7.cloned.1.call-done, bf16[512,1536]{1,0:T(8,128)(2,1)S(1)} %copy-done.5), kind=kOutput, calls=%fused_computation.73 | convolution fusion | flops 2418278400 | bytes 9437184 | tf_op jit(solution)/shard_map/dot_general | solution.py:89
  142.8 2.8 copy.69
  145.5 5.3 %all-to-all-start.1 = ((bf16[2,256,1536]{2,0,1:T(2,128)(2,1)}), bf16[2,256,1536]{2,0,1:T(2,128)(2,1)S(1)}, u32[]{:S(2)}, u32[]{:S(2)}) async-start(bf16[2,256,1536]{2,0,1:T(2,128)(2,1)} %copy.69), calls=%async_computation.1 | async-start | bytes 3145728 | tf_op jit(solution)/shard_map/all_to_all | solution.py:124
  153.4 25.1 %all-to-all-done.1 = bf16[2,256,1536]{2,0,1:T(2,128)(2,1)S(1)} async-done(((bf16[2,256,1536]{2,0,1:T(2,128)(2,1)}), bf16[2,256,1536]{2,0,1:T(2,128)(2,1)S(1)}, u32[]{:S(2)}, u32[]{:S(2)}) %all-to-all-start.1) | async-done | bytes 1572896 | tf_op jit(solution)/shard_map/all_to_all | solution.py:124
  185.0 34.7 %all-gather.9.cloned.1.call-done = bf16[1536,4608]{0,1:T(8,128)(2,1)} async-done(((bf16[1536,144]{0,1:T(8,128)(2,1)}), bf16[1536,4608]{0,1:T(8,128)(2,1)}) %all-gather.9.cloned.1.call-update) | async-done | bytes 14155792 | tf_op jit(solution)/shard_map/all_gather | solution.py:81
  219.6 10.7 %fusion.3 = bf16[64,8,4608]{2,1,0:T(8,128)(2,1)S(1)} fusion(bf16[512,1536]{1,0:T(8,128)(2,1)S(1)} %fusion.37, bf16[1536,4608]{0,1:T(8,128)(2,1)} %all-gather.9.cloned.1.call-done), kind=kOutput, calls=%fused_computation.8 | convolution fusion | flops 7250116608 | bytes 20447232 | tf_op jit(solution)/shard_map/dot_general | solution.py:79
  230.4 3.2 fusion.77
  233.6 5.5 %reshape.257 = f32[64,8,24,64]{3,2,1,0:T(8,128)} reshape(f32[64,8,1536]{2,1,0:T(8,128)} %get-tuple-element.20) | data formatting | bytes 6291456 | tf_op jit(solution)/shard_map/convert_element_type | solution.py:46
  239.1 5.2 %multiply_reduce_fusion = f32[64,8,24]{2,1,0:T(8,128)} fusion(f32[64,8,24,64]{3,2,1,0:T(8,128)} %reshape.257), kind=kLoop, calls=%fused_computation.22 | loop fusion | flops 1560576 | bytes 3194880 | tf_op jit(solution)/shard_map/reduce_sum | solution.py:17
  246.0 3.5 %reshape.256 = f32[64,8,24,64]{3,2,1,0:T(8,128)} reshape(f32[64,8,1536]{2,1,0:T(8,128)S(1)} %get-tuple-element.21) | data formatting | bytes 6291456 | tf_op jit(solution)/shard_map/convert_element_type | solution.py:45
  249.5 5.0 %multiply_reduce_fusion.1 = f32[64,8,24]{2,1,0:T(8,128)S(1)} fusion(f32[64,8,24,64]{3,2,1,0:T(8,128)} %reshape.256), kind=kLoop, calls=%fused_computation.27 | loop fusion | flops 1560576 | bytes 3194880 | tf_op jit(solution)/shard_map/reduce_sum | solution.py:17
  254.7 3.2 copy.73
  258.0 9.4 %fusion.7 = (f32[64,8,24,64]{3,0,2,1:T(8,128)S(1)}, f32[64,8,24,64]{3,0,2,1:T(8,128)S(1)}) fusion(f32[64,8,24,64]{3,2,1,0:T(8,128)} %reshape.257, f32[64]{0:T(128)S(1)} %get-tuple-element.37, f32[64,8,24]{0,2,1:T(8,128)S(1)} %add_rsqrt_fusion.1, f32[64]{0:T(128)S(1)} %get-tuple-element.40, f32[64,8,24]{0,2,1:T(8,128)S(1)} %add_rsqrt_fusion.2, ...), kind=kLoop, calls=%fused_computation.13 | loop fusion | flops 3145728 | bytes 12681728 | tf_op jit(solution)/shard_map/mul | solution.py:18
  267.4 7.9 %subtract_convert_fusion.3 = (bf16[64,8,24,16]{3,0,2,1:T(8,128)(2,1)}, bf16[64,8,24,16]{3,0,2,1:T(8,128)(2,1)}, bf16[64,8,24,16]{3,0,2,1:T(8,128)(2,1)}, bf16[64,8,24,16]{3,0,2,1:T(8,128)(2,1)}) fusion(f32[64,8,24,64]{3,0,2,1:T(8,128)S(1)} %get-tuple-element.58, f32[64,8,16]{2,0,1:T(8,128)S(1)} %copy-done.8, f32[64,8,16]{2,0,1:T(8,128)S(1)} %get-tuple-element.43, ...), kind=kLoop, calls=%fused_computation.26 | loop fusion | flops 3145728 | bytes 4849664 | tf_op jit(solution)/shard_map/convert.11
  275.4 7.8 %subtract_convert_fusion.1 = (bf16[64,8,24,16]{3,0,2,1:T(8,128)(2,1)}, bf16[64,8,24,16]{3,0,2,1:T(8,128)(2,1)}, bf16[64,8,24,16]{3,0,2,1:T(8,128)(2,1)}, bf16[64,8,24,16]{3,0,2,1:T(8,128)(2,1)}) fusion(f32[64,8,24,64]{3,0,2,1:T(8,128)S(1)} %get-tuple-element.57, f32[64,8,16]{2,0,1:T(8,128)S(1)} %copy-done.8, f32[64,8,16]{2,0,1:T(8,128)S(1)} %get-tuple-element.43, ...), kind=kLoop, calls=%fused_computation.21 | loop fusion | flops 3145728 | bytes 4849664 | tf_op jit(solution)/shard_map/convert.7
  283.1 12.9 %fusion.13 = (f32[8,24,64]{2,1,0:T(8,128)S(1)}, f32[8,24,64,64]{2,3,1,0:T(8,128)S(1)}) fusion(pred[8,64,64]{1,2,0:T(8,128)(4,1)S(1)} %broadcast_or_fusion.1, bf16[64,8,24,16]{3,0,2,1:T(8,128)(2,1)} %get-tuple-element.15, bf16[64,8,24,16]{3,0,2,1:T(8,128)(2,1)} %get-tuple-element.16, bf16[64,8,24,16]{3,0,2,1:T(8,128)(2,1)} %get-tuple-element.8, ...), kind=kOutput, calls=%fused_computation.32 | convolution fusion | flops 115593216 | bytes 6373376 | tf_op jit(solution)/shard_map/lbhd,mbhd->bhlm/dot_general | solution.py:58
  298.2 3.1 fusion.6
  301.3 5.3 %copy.80 = bf16[64,8,24,64]{3,2,1,0:T(8,128)(2,1)} copy(bf16[64,8,24,64]{0,3,2,1:T(8,128)(2,1)} %fusion.6) | data formatting | bytes 3145728 | tf_op jit(solution)/shard_map/convert_element_type | solution.py:73
  306.6 5.5 %convert_element_type.211 = bf16[512,1536]{1,0:T(8,128)(2,1)} reshape(bf16[64,8,24,64]{3,2,1,0:T(8,128)(2,1)} %copy.80) | data formatting | bytes 3145728 | tf_op jit(solution)/shard_map/convert_element_type | solution.py:73
  312.0 6.6 %fusion.45 = bf16[64,8,1536]{2,1,0:T(8,128)(2,1)} fusion(f32[512,1536]{1,0:T(8,128)S(1)} %bitcast.69, bf16[512,1536]{1,0:T(8,128)(2,1)} %convert_element_type.211, bf16[1536,1536]{0,1:T(8,128)(2,1)} %all-gather.11.cloned.1.call-done), kind=kOutput, calls=%fused_computation.74 | convolution fusion | flops 2417491968 | bytes 11010048 | tf_op jit(solution)/shard_map/dot_general | solution.py:89
  (87 shorter events, 25.7 us)
Async XLA Ops:
  6.5 11.9 %copy-start.13 = (s32[16384]{0:T(1024)S(1)}, s32[16384]{0:T(1024)}, u32[]{:S(2)}) copy-start(s32[16384]{0:T(1024)} %param.10) | copy-start | bytes 196612
  6.5 12.2 %copy-start.14 = (s32[64,256]{1,0:T(8,128)S(1)}, s32[64,256]{1,0:T(8,128)}, u32[]{:S(2)}) copy-start(s32[64,256]{1,0:T(8,128)} %param.11) | copy-start | bytes 196612
  6.5 12.3 %copy-start.15 = (f32[2,1536]{1,0:T(2,128)S(1)}, f32[2,1536]{1,0:T(2,128)}, u32[]{:S(2)}) copy-start(f32[2,1536]{1,0:T(2,128)} %param.12) | copy-start | bytes 36868
  6.5 12.3 %copy-start.16 = (f32[2,2,64]{2,1,0:T(2,128)S(1)}, f32[2,2,64]{2,1,0:T(2,128)}, u32[]{:S(2)}) copy-start(f32[2,2,64]{2,1,0:T(2,128)} %param.13) | copy-start | bytes 3076
  6.5 82.7 %all-gather.5.cloned.1.call-start = ((), (), s32[]{:S(2)}) async-start(), calls=%async_computation.2 | async-start | bytes 14598144 | tf_op jit(solution)/shard_map/all_gather | solution.py:81
  7.3 130.5 %all-gather.7.cloned.1.call-start = ((), (), s32[]{:S(2)}) async-start(), calls=%async_computation.3 | async-start | bytes 4866048 | tf_op jit(solution)/shard_map/all_gather | solution.py:91
  8.0 211.6 %all-gather.9.cloned.1.call-start = ((), (), s32[]{:S(2)}) async-start(), calls=%async_computation.4 | async-start | bytes 14598144 | tf_op jit(solution)/shard_map/all_gather | solution.py:81
  8.8 38.2 %all-to-all-start = ((bf16[32,16,1536]{2,1,0:T(8,128)(2,1)}), bf16[32,16,1536]{2,1,0:T(8,128)(2,1)S(1)}, u32[]{:S(2)}, u32[]{:S(2)}) async-start(bf16[32,16,1536]{2,1,0:T(8,128)(2,1)} %bitcast.73), calls=%async_computation | async-start | bytes 3145728 | tf_op jit(solution)/shard_map/all_to_all | solution.py:104
  50.4 50.0 %copy-start.4 = (bf16[512,1536]{1,0:T(8,128)(2,1)}, bf16[512,1536]{1,0:T(8,128)(2,1)S(1)}, u32[]{:S(2)}) copy-start(bf16[512,1536]{1,0:T(8,128)(2,1)S(1)} %scatter_custom_fusion) | copy-start | bytes 4718596
  110.9 2.9 copy-start
  118.5 3.1 copy-start.11
  125.1 12.6 %copy-start.5 = (bf16[512,1536]{1,0:T(8,128)(2,1)S(1)}, bf16[512,1536]{1,0:T(8,128)(2,1)}, u32[]{:S(2)}) copy-start(bf16[512,1536]{1,0:T(8,128)(2,1)} %copy-done.4) | copy-start | bytes 4718596
  145.5 33.0 %all-to-all-start.1 = ((bf16[2,256,1536]{2,0,1:T(2,128)(2,1)}), bf16[2,256,1536]{2,0,1:T(2,128)(2,1)S(1)}, u32[]{:S(2)}, u32[]{:S(2)}) async-start(bf16[2,256,1536]{2,0,1:T(2,128)(2,1)} %copy.69), calls=%async_computation.1 | async-start | bytes 3145728 | tf_op jit(solution)/shard_map/all_to_all | solution.py:124
  150.9 161.2 %all-gather.11.cloned.1.call-start = ((), (), s32[]{:S(2)}) async-start(), calls=%async_computation.5 | async-start | bytes 4866048 | tf_op jit(solution)/shard_map/all_gather | solution.py:91
  249.5 5.1 %copy-start.6 = (bf16[64,8,1536]{2,1,0:T(8,128)(2,1)S(1)}, bf16[64,8,1536]{2,1,0:T(8,128)(2,1)}, u32[]{:S(2)}) copy-start(bf16[64,8,1536]{2,1,0:T(8,128)(2,1)} %get-tuple-element.19) | copy-start | bytes 4718596
  254.5 3.4 %copy-start.12 = (f32[64,8,24]{0,2,1:T(8,128)S(1)}, f32[64,8,24]{0,2,1:T(8,128)}, u32[]{:S(2)}) copy-start(f32[64,8,24]{0,2,1:T(8,128)} %copy.77) | copy-start | bytes 147460
  258.0 9.5 %copy-start.8 = (f32[64,8,16]{2,0,1:T(8,128)S(1)}, f32[64,8,16]{2,0,1:T(8,128)}, u32[]{:S(2)}) copy-start(f32[64,8,16]{2,0,1:T(8,128)} %get-tuple-element.44) | copy-start | bytes 98308
  258.0 9.5 %copy-start.9 = (f32[64,8,16]{2,0,1:T(8,128)S(1)}, f32[64,8,16]{2,0,1:T(8,128)}, u32[]{:S(2)}) copy-start(f32[64,8,16]{2,0,1:T(8,128)} %get-tuple-element.49) | copy-start | bytes 98308
  258.0 9.5 %copy-start.10 = (f32[64,8,16]{2,0,1:T(8,128)S(1)}, f32[64,8,16]{2,0,1:T(8,128)}, u32[]{:S(2)}) copy-start(f32[64,8,16]{2,0,1:T(8,128)} %get-tuple-element.50) | copy-start | bytes 98308
  275.4 7.8 %copy-start.1 = (bf16[64,8,24,16]{3,0,2,1:T(8,128)(2,1)S(1)}, bf16[64,8,24,16]{3,0,2,1:T(8,128)(2,1)}, u32[]{:S(2)}) copy-start(bf16[64,8,24,16]{3,0,2,1:T(8,128)(2,1)} %get-tuple-element.11) | copy-start | bytes 1179652
  275.4 7.8 %copy-start.2 = (bf16[64,8,24,16]{3,0,2,1:T(8,128)(2,1)S(1)}, bf16[64,8,24,16]{3,0,2,1:T(8,128)(2,1)}, u32[]{:S(2)}) copy-start(bf16[64,8,24,16]{3,0,2,1:T(8,128)(2,1)} %get-tuple-element.12) | copy-start | bytes 1179652
  296.1 2.1 copy-start.7
  306.6 5.5 %copy-start.3 = (f32[2,32,8,1536]{3,2,0,1:T(8,128)S(1)}, f32[2,32,8,1536]{3,2,0,1:T(8,128)}, u32[]{:S(2)}) copy-start(f32[2,32,8,1536]{3,2,0,1:T(8,128)} %copy.70) | copy-start | bytes 9437188
Sparse Core Ops, SparseCore 0:
  9.6 79.6 all-gather.4
  91.5 46.2 all-gather.6
  140.0 79.5 all-gather.8
  221.7 46.2 all-gather.10
where the time goes:
time: 330 us; the launch traced here: 325 us
  waiting for transfers between devices  139 us (42%)
  other arithmetic  58.9 us (18%)
  matrix products  55.3 us (17%)
  local copies, waits for them, and re-layouts  43.2 us (13%)
  starting transfers between devices  15.1 us (5%)
  between operations  13.8 us (4%)
    all_gather x2, waiting for transfers between devices, project_qkv(): lax.all_gather(weight, 'fsdp', axis=1, tiled=True)  73.2 us
    all_to_all x1, waiting for transfers between devices, on_device(): lax.all_to_all(tiles.reshape(count, slots, width), 'fsdp', split_axis=0,...  27.7 us
    all_to_all x1, waiting for transfers between devices, on_device(): lax.all_to_all(hidden, 'fsdp', split_axis=1, concat_axis=0, tiled=True)  25.1 us
    dot_general x2, matrix products, multiply(): return jnp.dot(normed, piece, preferred_element_type=jnp.float32)  21.8 us
    another operation x4, other arithmetic  16.8 us
    dot_general x2, matrix products, attend(): jnp.einsum(score_form, query, key, preferred_element_type=jnp.float32)  15.3 us
    reduce_sum x4, other arithmetic, head_norm(): scale = lax.rsqrt(jnp.mean(values * values, axis=-1, keepdims=True) + EPS)  13.1 us
    convert_element_type x3, local copies, waits for them, and re-layouts, attend(): (mixed / total[..., None]).reshape(qkv.shape[:-1] + (width,))  12.4 us
  transfers between devices with their start and end apart: 6, of which 5 were waited for; matrix products, arithmetic and copies ran while one was open for 46% of the time, Pallas kernels for 0%

commit v1 on v0

--- a/solution.py
+++ b/solution.py
@@ -78,9 +78,12 @@
     def multiply(piece, start):
         return jnp.dot(normed, piece, preferred_element_type=jnp.float32)
 
-    return multiply(lax.all_gather(weight, "fsdp", axis=1, tiled=True), jnp.int32(0)).astype(
-        jnp.bfloat16
-    )
+    return multiply(
+        jnp.concatenate(
+            lax.all_to_all(jnp.stack([weight] * lax.axis_size("fsdp")), "fsdp", 0, 0), axis=1
+        ),
+        jnp.int32(0),
+    ).astype(jnp.bfloat16)
 
 
 def project_out(mixed, weight):

time: 330 us -> 618 us (1.87)
  the two profiles are of different devices: /device:TPU:1 before, /device:TPU:0 now
where the time goes in v1:
time: 618 us; the launch traced here: 612 us
  waiting for transfers between devices  363 us (59%)
  other arithmetic  59.3 us (10%)
  blocking collectives  57.9 us (9%)
  matrix products  54.5 us (9%)
  local copies, waits for them, and re-layouts  52.8 us (9%)
  between operations  14.2 us (2%)
  starting transfers between devices  10.4 us (2%)
    all_to_all x2, waiting for transfers between devices, project_qkv(): lax.all_to_all(jnp.stack([weight] * lax.axis_size('fsdp')), 'fsdp', 0, 0)  361 us
    all_to_all x1, blocking collectives, on_device(): lax.all_to_all(tiles.reshape(count, slots, width), 'fsdp', split_axis=0,...  31.4 us
    all_to_all x1, blocking collectives, on_device(): lax.all_to_all(hidden, 'fsdp', split_axis=1, concat_axis=0, tiled=True)  26.5 us
    dot_general x2, matrix products, multiply(): return jnp.dot(normed, piece, preferred_element_type=jnp.float32)  22.3 us
    another operation x4, other arithmetic  16.7 us
    dot_general x2, matrix products, attend(): jnp.einsum(score_form, query, key, preferred_element_type=jnp.float32)  15.3 us
    another operation x2, local copies, waits for them, and re-layouts, project_qkv(): jnp.stack([weight] * lax.axis_size('fsdp'))  13.5 us
    reduce_sum x4, other arithmetic, head_norm(): scale = lax.rsqrt(jnp.mean(values * values, axis=-1, keepdims=True) + EPS)  12.7 us
  transfers between devices with their start and end apart: 4, of which 2 were waited for; matrix products, arithmetic and copies ran while one was open for 23% of the time, Pallas kernels for 0%

profile of v1, /device:TPU:0, one launch (start us, length us, event | category | flops | bytes accessed | tf_op | source)
XLA Modules:
  0.0 611.9 jit_solution(7815009994998030511)
XLA Ops:
  6.5 31.4 %all_to_all.24 = bf16[32,16,1536]{2,1,0:T(8,128)(2,1)S(1)} all-to-all(bf16[32,16,1536]{2,1,0:T(8,128)(2,1)} %bitcast.79), channel_id=1, replica_groups=mesh['fsdp'=32,'slide'=4] {'fsdp'}, dimensions={0} | all-to-all | bytes 3145728 | tf_op jit(solution)/shard_map/all_to_all | solution.py:107
  37.9 6.7 %stack.4 = bf16[32,1536,144]{1,2,0:T(8,128)(2,1)} broadcast(bf16[1536,144]{0,1:T(8,128)(2,1)S(1)} %copy-done.12), dimensions={1,2} | broadcast | bytes 14598144 | tf_op jit(solution)/shard_map/stack | solution.py:83
  44.7 5.2 all-to-all-start.1
  51.6 3.4 scatter_custom_fusion
  55.4 181.9 %all-to-all-done.1 = bf16[32,1536,144]{1,2,0:T(8,128)(2,1)} async-done(((bf16[32,1536,144]{1,2,0:T(8,128)(2,1)}), bf16[32,1536,144]{1,2,0:T(8,128)(2,1)}, u32[]{:S(2)}, u32[]{:S(2)}) %all-to-all-start.1) | async-done | bytes 14155808 | tf_op jit(solution)/shard_map/all_to_all | solution.py:83
  237.3 11.1 %convolution_convert_fusion.1 = bf16[512,4608]{1,0:T(8,128)(2,1)S(1)} fusion(bf16[1536,4608]{0,1:T(8,128)(2,1)} %bitcast.4, bf16[512,1536]{1,0:T(8,128)(2,1)S(1)} %scatter_custom_fusion, f32[1536]{0:T(1024)S(1)} %get-tuple-element.6, f32[512]{0:T(512)S(1)} %add_rsqrt_fusion.5), kind=kOutput, calls=%fused_computation.7 | convolution fusion | flops 7253262336 | bytes 20455424 | tf_op jit(solution)/shard_map/dot_general | solution.py:79
  248.4 3.2 slice_convert_fusion.2
  253.9 2.4 copy.65
  256.3 2.6 copy.63
  258.9 2.5 multiply_reduce_fusion.3
  266.5 3.1 fusion.1
  269.7 3.5 fusion.39
  275.2 5.0 fusion.45
  281.8 26.5 %all_to_all.25 = bf16[2,256,1536]{2,0,1:T(2,128)(2,1)} all-to-all(bf16[2,256,1536]{2,0,1:T(2,128)(2,1)S(1)} %copy.68), channel_id=1, replica_groups=mesh['fsdp'=32,'slide'=4] {'fsdp'}, dimensions={1} | all-to-all | bytes 3145728 | tf_op jit(solution)/shard_map/all_to_all | solution.py:127
  308.3 6.7 %stack.5 = bf16[32,1536,144]{1,2,0:T(8,128)(2,1)} broadcast(bf16[1536,144]{0,1:T(8,128)(2,1)S(1)} %copy-done.13), dimensions={1,2} | broadcast | bytes 14598144 | tf_op jit(solution)/shard_map/stack | solution.py:83
  315.0 5.1 all-to-all-start.3
  322.9 2.7 bitcast_convert_fusion
  328.0 179.6 %all-to-all-done.3 = bf16[32,1536,144]{1,2,0:T(8,128)(2,1)} async-done(((bf16[32,1536,144]{1,2,0:T(8,128)(2,1)}), bf16[32,1536,144]{1,2,0:T(8,128)(2,1)}, u32[]{:S(2)}, u32[]{:S(2)}) %all-to-all-start.3) | async-done | bytes 14155808 | tf_op jit(solution)/shard_map/all_to_all | solution.py:83
  507.6 11.2 %fusion.3 = bf16[64,8,4608]{2,1,0:T(8,128)(2,1)S(1)} fusion(bf16[512,1536]{1,0:T(8,128)(2,1)} %bitcast.84, bf16[1536,4608]{0,1:T(8,128)(2,1)} %bitcast.19), kind=kOutput, calls=%fused_computation.8 | convolution fusion | flops 7250116608 | bytes 20447232 | tf_op jit(solution)/shard_map/dot_general | solution.py:79
  518.7 3.2 fusion.78
  521.9 5.5 reshape.279
  527.3 5.2 multiply_reduce_fusion
  534.3 3.5 reshape.278
  537.8 4.6 multiply_reduce_fusion.1
  542.5 3.2 copy.72
  545.8 9.3 %fusion.7 = (f32[64,8,24,64]{3,0,2,1:T(8,128)S(1)}, f32[64,8,24,64]{3,0,2,1:T(8,128)S(1)}) fusion(f32[64,8,24,64]{3,2,1,0:T(8,128)} %reshape.279, f32[64]{0:T(128)S(1)} %get-tuple-element.37, f32[64,8,24]{0,2,1:T(8,128)S(1)} %add_rsqrt_fusion, f32[64]{0:T(128)S(1)} %get-tuple-element.40, f32[64,8,24]{0,2,1:T(8,128)S(1)} %add_rsqrt_fusion.1, ...), kind=kLoop, calls=%fused_computation.13 | loop fusion | flops 3145728 | bytes 12681728 | tf_op jit(solution)/shard_map/mul | solution.py:18
  555.1 7.9 %subtract_convert_fusion.3 = (bf16[64,8,24,16]{3,0,2,1:T(8,128)(2,1)}, bf16[64,8,24,16]{3,0,2,1:T(8,128)(2,1)}, bf16[64,8,24,16]{3,0,2,1:T(8,128)(2,1)}, bf16[64,8,24,16]{3,0,2,1:T(8,128)(2,1)}) fusion(f32[64,8,24,64]{3,0,2,1:T(8,128)S(1)} %get-tuple-element.58, f32[64,8,16]{2,0,1:T(8,128)S(1)} %copy-done.8, f32[64,8,16]{2,0,1:T(8,128)S(1)} %get-tuple-element.43, ...), kind=kLoop, calls=%fused_computation.26 | loop fusion | flops 3145728 | bytes 4849664 | tf_op jit(solution)/shard_map/convert.13
  563.0 7.8 %subtract_convert_fusion.1 = (bf16[64,8,24,16]{3,0,2,1:T(8,128)(2,1)}, bf16[64,8,24,16]{3,0,2,1:T(8,128)(2,1)}, bf16[64,8,24,16]{3,0,2,1:T(8,128)(2,1)}, bf16[64,8,24,16]{3,0,2,1:T(8,128)(2,1)}) fusion(f32[64,8,24,64]{3,0,2,1:T(8,128)S(1)} %get-tuple-element.57, f32[64,8,16]{2,0,1:T(8,128)S(1)} %copy-done.8, f32[64,8,16]{2,0,1:T(8,128)S(1)} %get-tuple-element.43, ...), kind=kLoop, calls=%fused_computation.21 | loop fusion | flops 3145728 | bytes 4849664 | tf_op jit(solution)/shard_map/convert.9
  570.8 13.0 %fusion.13 = (f32[8,24,64]{2,1,0:T(8,128)S(1)}, f32[8,24,64,64]{2,3,1,0:T(8,128)S(1)}) fusion(pred[8,64,64]{1,2,0:T(8,128)(4,1)S(1)} %broadcast_or_fusion.1, bf16[64,8,24,16]{3,0,2,1:T(8,128)(2,1)} %get-tuple-element.15, bf16[64,8,24,16]{3,0,2,1:T(8,128)(2,1)} %get-tuple-element.16, bf16[64,8,24,16]{3,0,2,1:T(8,128)(2,1)} %get-tuple-element.8, ...), kind=kOutput, calls=%fused_computation.32 | convolution fusion | flops 115593216 | bytes 6373376 | tf_op jit(solution)/shard_map/lbhd,mbhd->bhlm/dot_general | solution.py:58
  587.9 3.8 copy.79
  591.7 4.5 convert_element_type.216
  598.3 6.5 %fusion.46 = bf16[64,8,1536]{2,1,0:T(8,128)(2,1)} fusion(f32[512,1536]{1,0:T(8,128)} %bitcast.78, bf16[512,1536]{1,0:T(8,128)(2,1)S(1)} %convert_element_type.216, bf16[1536,1536]{0,1:T(8,128)(2,1)} %all-gather.5.cloned.1.call-done), kind=kOutput, calls=%fused_computation.75 | convolution fusion | flops 2417491968 | bytes 11010048 | tf_op jit(solution)/shard_map/dot_general | solution.py:92
  (90 shorter events, 26.3 us)
Async XLA Ops:
  6.5 31.4 %copy-start.12 = (bf16[1536,144]{0,1:T(8,128)(2,1)S(1)}, bf16[1536,144]{0,1:T(8,128)(2,1)}, u32[]{:S(2)}) copy-start(bf16[1536,144]{0,1:T(8,128)(2,1)} %param.14) | copy-start | bytes 1327108
  44.7 6.0 copy-start.15
  44.7 6.4 %copy-start.16 = (s32[64,256]{1,0:T(8,128)S(1)}, s32[64,256]{1,0:T(8,128)}, u32[]{:S(2)}) copy-start(s32[64,256]{1,0:T(8,128)} %param.11) | copy-start | bytes 196612
  44.7 6.4 %copy-start.18 = (f32[2,2,64]{2,1,0:T(2,128)S(1)}, f32[2,2,64]{2,1,0:T(2,128)}, u32[]{:S(2)}) copy-start(f32[2,2,64]{2,1,0:T(2,128)} %param.13) | copy-start | bytes 3076
  44.7 6.5 %copy-start.17 = (f32[2,1536]{1,0:T(2,128)S(1)}, f32[2,1536]{1,0:T(2,128)}, u32[]{:S(2)}) copy-start(f32[2,1536]{1,0:T(2,128)} %param.12) | copy-start | bytes 36868
  44.7 192.6 %all-to-all-start.1 = ((bf16[32,1536,144]{1,2,0:T(8,128)(2,1)}), bf16[32,1536,144]{1,2,0:T(8,128)(2,1)}, u32[]{:S(2)}, u32[]{:S(2)}) async-start(bf16[32,1536,144]{1,2,0:T(8,128)(2,1)} %stack.4), calls=%async_computation.1 | async-start | bytes 28311552 | tf_op jit(solution)/shard_map/all_to_all | solution.py:83
  49.9 225.2 %all-gather.3.cloned.1.call-start = ((), (), s32[]{:S(2)}) async-start(), calls=%async_computation.4 | async-start | bytes 4866048 | tf_op jit(solution)/shard_map/all_gather | solution.py:94
  55.0 193.4 %copy-start.4 = (bf16[512,1536]{1,0:T(8,128)(2,1)}, bf16[512,1536]{1,0:T(8,128)(2,1)S(1)}, u32[]{:S(2)}) copy-start(bf16[512,1536]{1,0:T(8,128)(2,1)S(1)} %scatter_custom_fusion) | copy-start | bytes 4718596
  258.9 2.9 copy-start
  266.5 3.1 copy-start.11
  273.1 2.0 copy-start.5
  280.2 28.1 %copy-start.13 = (bf16[1536,144]{0,1:T(8,128)(2,1)S(1)}, bf16[1536,144]{0,1:T(8,128)(2,1)}, u32[]{:S(2)}) copy-start(bf16[1536,144]{0,1:T(8,128)(2,1)} %param.16) | copy-start | bytes 1327108
  315.0 192.5 %all-to-all-start.3 = ((bf16[32,1536,144]{1,2,0:T(8,128)(2,1)}), bf16[32,1536,144]{1,2,0:T(8,128)(2,1)}, u32[]{:S(2)}, u32[]{:S(2)}) async-start(bf16[32,1536,144]{1,2,0:T(8,128)(2,1)} %stack.5), calls=%async_computation.3 | async-start | bytes 28311552 | tf_op jit(solution)/shard_map/all_to_all | solution.py:83
  320.1 278.2 %all-gather.5.cloned.1.call-start = ((), (), s32[]{:S(2)}) async-start(), calls=%async_computation.5 | async-start | bytes 4866048 | tf_op jit(solution)/shard_map/all_gather | solution.py:94
  537.8 4.8 copy-start.6
  542.4 3.4 copy-start.14
  545.8 9.3 %copy-start.8 = (f32[64,8,16]{2,0,1:T(8,128)S(1)}, f32[64,8,16]{2,0,1:T(8,128)}, u32[]{:S(2)}) copy-start(f32[64,8,16]{2,0,1:T(8,128)} %get-tuple-element.44) | copy-start | bytes 98308
  545.8 9.3 %copy-start.9 = (f32[64,8,16]{2,0,1:T(8,128)S(1)}, f32[64,8,16]{2,0,1:T(8,128)}, u32[]{:S(2)}) copy-start(f32[64,8,16]{2,0,1:T(8,128)} %get-tuple-element.49) | copy-start | bytes 98308
  545.8 9.3 %copy-start.10 = (f32[64,8,16]{2,0,1:T(8,128)S(1)}, f32[64,8,16]{2,0,1:T(8,128)}, u32[]{:S(2)}) copy-start(f32[64,8,16]{2,0,1:T(8,128)} %get-tuple-element.50) | copy-start | bytes 98308
  563.0 7.8 %copy-start.2 = (bf16[64,8,24,16]{3,0,2,1:T(8,128)(2,1)S(1)}, bf16[64,8,24,16]{3,0,2,1:T(8,128)(2,1)}, u32[]{:S(2)}) copy-start(bf16[64,8,24,16]{3,0,2,1:T(8,128)(2,1)} %get-tuple-element.11) | copy-start | bytes 1179652
  563.0 7.8 %copy-start.3 = (bf16[64,8,24,16]{3,0,2,1:T(8,128)(2,1)S(1)}, bf16[64,8,24,16]{3,0,2,1:T(8,128)(2,1)}, u32[]{:S(2)}) copy-start(bf16[64,8,24,16]{3,0,2,1:T(8,128)(2,1)} %get-tuple-element.12) | copy-start | bytes 1179652
  583.7 2.2 copy-start.7
  591.7 4.5 copy-start.1
Sparse Core Ops, SparseCore 0:
  53.0 167.7 all-gather.2
  323.2 167.7 all-gather.4
